TPU v7x, 512 devices: a whole 4x8x8 slice. The times are simulated.
512 devices in a mesh: ctx: 32 (over z, y_hi, core), fsdp: 16 (over y_lo, x).
Axes of the slice: x: 4, y: 8 (y_hi: 2, y_lo: 4; y = y_hi * 4 + y_lo), z: 8, core: 2. Of those that a mesh axis runs over, the one named last changes fastest.
Arguments:
- tokens: bfloat16 [16384, 8192], P('ctx', 'fsdp'), may hold values from -6 to 6
- gain: float32 [8192], replicated, may hold values from 0.5 to 1.5
- in_weight: bfloat16 [8192, 3, 4096], P('ctx', None, 'fsdp'), may hold values from -0.0625 to 0.0625
- short_filter: float32 [3, 3, 4096], P(None, None, 'fsdp'), may hold values from -3.5 to 3.5
- long_filter: float32 [128, 4096], P(None, 'fsdp'), may hold values from -0.5 to 0.5
Outputs:
- gated_out: bfloat16 [16384, 4096], P('ctx', 'fsdp')
All inputs are finite; a program needn't handle non-finite values.
Results may differ from a plain program's by a relative error of at most 0.0086.
Values may be sent and summed in bfloat16 or wider, within the bound.
A program may use at most 64 MiB of HBM per device.

v0:
```python
import jax
import jax.numpy as jnp
from jax import lax
from jax.sharding import PartitionSpec as P


def passed_along(value, axis, steps):
    count = lax.axis_size(axis)
    leading, last = (max(0, -steps), min(count, count - steps))
    return lax.ppermute(value, axis, [(source, source + steps) for source in range(leading, last)])


def short_mix(extended_rows, short_taps, row_count):
    extended = extended_rows.astype(jnp.float32)
    tap_count = short_taps.shape[0]
    result = jnp.zeros((row_count, extended.shape[1]), jnp.float32)
    for offset in range(tap_count):
        result = (
            result
            + short_taps[offset]
            * extended[tap_count - 1 - offset : tap_count - 1 - offset + row_count]
        )
    return result


def long_mix(signal_rows, filters, row_count):
    signal = signal_rows.astype(jnp.float32)
    tap_count = filters.shape[0]

    def group_step(counter, accumulated):
        for within in range(16):
            lag_value = counter * 16 + within
            window_rows = lax.dynamic_slice_in_dim(signal, tap_count - 1 - lag_value, row_count, 0)
            tap_weights = lax.dynamic_slice_in_dim(filters, lag_value, 1, 0)
            accumulated = accumulated + tap_weights * window_rows
        return accumulated

    initial = jnp.zeros((row_count, signal.shape[1]), jnp.float32)
    return lax.fori_loop(0, tap_count // 16, group_step, initial)


def on_device(tokens, gain, in_weight, short_filter, long_filter):
    row_count = tokens.shape[0]
    features = lax.all_gather(tokens, "fsdp", axis=1, tiled=True)
    widened = features.astype(jnp.float32)
    mean_square = jnp.mean(widened * widened, axis=1, keepdims=True)
    normed = (widened * lax.rsqrt(mean_square + 1e-06) * gain).astype(jnp.bfloat16)
    channels = in_weight.shape[2]
    panel_rows = lax.all_gather(in_weight, "ctx", axis=0, tiled=True)
    projected = jnp.dot(
        normed,
        panel_rows.reshape(panel_rows.shape[0], 3 * channels),
        preferred_element_type=jnp.float32,
    )
    projected = projected.astype(jnp.bfloat16)
    short_taps = short_filter.reshape(short_filter.shape[0], 3 * channels)
    short_count = short_taps.shape[0]
    long_count = long_filter.shape[0]
    upper_rim = passed_along(projected[row_count - (short_count - 1) :], "ctx", 1)
    featurized = short_mix(jnp.concatenate([upper_rim, projected], axis=0), short_taps, row_count)
    query = featurized[:, :channels]
    gated = (featurized[:, channels : 2 * channels] * featurized[:, 2 * channels :]).astype(
        jnp.bfloat16
    )
    gated_rim = passed_along(gated[row_count - (long_count - 1) :], "ctx", 1)
    signal_rows = jnp.concatenate([gated_rim, gated], axis=0)
    response = long_mix(signal_rows, long_filter, row_count)
    return (query * response).astype(jnp.bfloat16)


def solution(mesh):
    return jax.shard_map(
        on_device,
        mesh=mesh,
        in_specs=(
            P("ctx", "fsdp"),
            P(),
            P("ctx", None, "fsdp"),
            P(None, None, "fsdp"),
            P(None, "fsdp"),
        ),
        out_specs=P("ctx", "fsdp"),
        check_vma=False,
    )
```

profile of v0, /device:TPU:1, one launch (start us, length us, event | category | flops | bytes accessed | tf_op | source)
XLA Modules:
  0.0 353.8 jit_solution(12686480157825419753)
XLA Ops:
  7.3 1.9 copy.6
  9.3 110.7 %all-gather.3.cloned.1.call-done = bf16[512,8192]{1,0:T(8,128)(2,1)} async-done(((bf16[512,512]{1,0:T(8,128)(2,1)}), bf16[512,8192]{1,0:T(8,128)(2,1)}) %all-gather.3.cloned.1.call-update) | async-done | bytes 8388624 | tf_op jit(solution)/shard_map/all_gather | solution.py:44
  120.0 5.1 %fusion.15 = f32[512]{0:T(512)S(1)} fusion(bf16[512,8192]{1,0:T(8,128)(2,1)} %all-gather.3.cloned.1.call-done), kind=kLoop, calls=%fused_computation.34 | loop fusion | flops 12582400 | bytes 8390656 | tf_op jit(solution)/shard_map/reduce_sum | solution.py:46
  125.1 171.7 %all-gather.5.cloned.1.call-done = bf16[8192,3,256]{0,2,1:T(8,128)(2,1)} async-done(((bf16[256,3,256]{0,2,1:T(8,128)(2,1)}), bf16[8192,3,256]{0,2,1:T(8,128)(2,1)}) %all-gather.5.cloned.1.call-update) | async-done | bytes 12582928 | tf_op jit(solution)/shard_map/all_gather | solution.py:49
  296.8 13.1 %fusion.24 = bf16[512,768]{1,0:T(8,128)(2,1)S(1)} fusion(bf16[8192,768]{0,1:T(8,128)(2,1)} %bitcast.66, bf16[512,8192]{1,0:T(8,128)(2,1)} %all-gather.3.cloned.1.call-done, f32[8192]{0:T(1024)S(1)} %copy-done.1, f32[512]{0:T(512)S(1)} %add_rsqrt_fusion), kind=kOutput, calls=%fused_computation.45 | convolution fusion | flops 6459621376 | bytes 21792768 | tf_op jit(solution)/shard_map/dot_general | solution.py:50
  309.9 1.9 collective-permute-start
  313.7 7.7 %collective-permute-start.1 = (bf16[127,256]{1,0:T(8,128)(2,1)S(1)}, bf16[127,256]{1,0:T(8,128)(2,1)S(1)}, u32[]{:S(2)}, u32[]{:S(2)}) collective-permute-start(bf16[127,256]{1,0:T(8,128)(2,1)S(1)} %slice.54), channel_id=1, source_target_pairs={{0,16},{16,32},{32,48},{48,64},{64,80},{80,96},{96,112},{112,128},... | collective-permute-start | bytes 195080 | tf_op jit(solution)/shard_map/ppermute | solution.py:10
  321.4 1.3 collective-permute-done.1
  322.8 23.4 %while.17 = (s32[]{:T(128)}, f32[512,256]{1,0:T(8,128)S(1)}, f32[128,256]{1,0:T(8,128)}, f32[639,256]{1,0:T(8,128)S(1)}, s32[]{:T(128)}, /*index=5*/s32[]{:T(128...) while((s32[]{:T(128)}, f32[512,256]{1,0:T(8,128)S(1)}, ...), condition=%wide.region_2.0_spmd.clone, body=%wide.region_1.0_spmd.clone.sunk | while | flops 4325507 | bytes 9488279 | solution.py:39
  322.9 1.1 constant_dynamic-slice_fusion.17
  324.1 1.6 fusion.32
  325.8 1.1 constant_dynamic-slice_fusion.17
  327.0 1.6 fusion.32
  328.7 1.1 constant_dynamic-slice_fusion.17
  330.0 1.6 fusion.32
  331.7 1.1 constant_dynamic-slice_fusion.17
  332.9 1.6 fusion.32
  334.6 1.1 constant_dynamic-slice_fusion.17
  335.8 1.6 fusion.32
  337.5 1.1 constant_dynamic-slice_fusion.17
  338.7 1.6 fusion.32
  341.7 1.6 fusion.32
  343.4 1.1 constant_dynamic-slice_fusion.17
  344.6 1.6 fusion.32
  (23 shorter events, 4.5 us)
Async XLA Ops:
  6.5 113.5 %all-gather.3.cloned.1.call-start = ((), (), s32[]{:S(2)}) async-start(), calls=%async_computation | async-start | bytes 8912896 | tf_op jit(solution)/shard_map/all_gather | solution.py:44
  7.3 289.5 %all-gather.5.cloned.1.call-start = ((), (), s32[]{:S(2)}) async-start(), calls=%async_computation.1 | async-start | bytes 12976128 | tf_op jit(solution)/shard_map/all_gather | solution.py:49
  9.2 287.5 %copy-start.1 = (f32[8192]{0:T(1024)S(1)}, f32[8192]{0:T(1024)}, u32[]{:S(2)}) copy-start(f32[8192]{0:T(1024)} %param.8) | copy-start | bytes 98308
  296.8 15.1 %copy-start = (f32[3,3,256]{2,1,0:T(4,128)S(1)}, f32[3,3,256]{2,1,0:T(4,128)}, u32[]{:S(2)}) copy-start(f32[3,3,256]{2,1,0:T(4,128)} %param.10) | copy-start | bytes 27652
  309.9 3.1 collective-permute-start
  313.7 9.0 %collective-permute-start.1 = (bf16[127,256]{1,0:T(8,128)(2,1)S(1)}, bf16[127,256]{1,0:T(8,128)(2,1)S(1)}, u32[]{:S(2)}, u32[]{:S(2)}) collective-permute-start(bf16[127,256]{1,0:T(8,128)(2,1)S(1)} %slice.54), channel_id=1, source_target_pairs={{0,16},{16,32},{32,48},{48,64},{64,80},{80,96},{96,112},{112,128},... | collective-permute-start | bytes 195080 | tf_op jit(solution)/shard_map/ppermute | solution.py:10
Sparse Core Ops, SparseCore 0:
  9.4 110.5 all-gather.2
  123.1 173.5 all-gather.4
where the time goes:
time: 361 us; the launch traced here: 354 us
  waiting for transfers between devices  285 us (79%)
  other arithmetic  19.3 us (5%)
  between operations  13.5 us (4%)
  matrix products  13.1 us (4%)
  local copies, waits for them, and re-layouts  10.6 us (3%)
  starting transfers between devices  9.65 us (3%)
    all_gather x1, waiting for transfers between devices, on_device(): panel_rows = lax.all_gather(in_weight, 'ctx', axis=0, tiled=True)  172 us
    all_gather x1, waiting for transfers between devices, on_device(): features = lax.all_gather(tokens, 'fsdp', axis=1, tiled=True)  111 us
    dot_general x1, matrix products, on_device(): jnp.dot(normed, panel_rows.reshape(panel_rows.shape[0], 3 * channels), pr...  13.1 us
    add x8, other arithmetic, group_step(): accumulated = accumulated + tap_weights * window_rows  12.7 us
    ppermute x2, starting transfers between devices, passed_along(): lax.ppermute(value, axis, [(source, source + steps) for source in range(l...  9.61 us
    dynamic_slice x8, local copies, waits for them, and re-layouts, group_step(): tap_weights = lax.dynamic_slice_in_dim(filters, lag_value, 1, 0)  8.62 us
  transfers between devices with their start and end apart: 4, of which 4 were waited for; matrix products, arithmetic and copies ran while one was open for 2% of the time, Pallas kernels for 0%

commit v1 on v0

v1 whole, which is shorter than its diff:
```python
import jax
import jax.numpy as jnp
from jax import lax
from jax.experimental import pallas as pl
from jax.experimental.pallas import tpu as pltpu
from jax.sharding import PartitionSpec as P

MESH = pl.DeviceIdType.MESH
F32 = jnp.float32
BF16 = jnp.bfloat16

ROWS, FEATS, KROWS, CHAN = 512, 512, 256, 256
TAPS, SHORT = 128, 3


def kernel(tok, gain, w, sfilt, lfilt, out, tall, wall, acc, ssq, pf, gext, gsh, gsend, psend, grecv, precv,
           lsem, tss, trs, wss, wrs, hss, hrs):
    ctx = lax.axis_index("ctx")
    fsdp = lax.axis_index("fsdp")
    core = ctx % 2
    hi = (ctx // 2) % 2
    z = ctx // 4
    x = fsdp % 4
    lo = fsdp // 4

    def at(xx, ll, hh, zz, cc):
        return ((zz * 2 + hh) * 2 + cc, ll * 4 + xx)

    xp, xm = at((x + 1) % 4, lo, hi, z, core), at((x + 3) % 4, lo, hi, z, core)
    zp, zm = at(x, lo, hi, (z + 1) % 8, core), at(x, lo, hi, (z + 7) % 8, core)
    y = hi * 4 + lo
    yp = at(x, (y + 1) % 8 % 4, (y + 1) % 8 // 4, z, core)
    ym = at(x, (y + 7) % 8 % 4, (y + 7) % 8 // 4, z, core)
    partner = at(x, lo, 1 - hi, z, core)
    sibling = at(x, lo, hi, z, 1 - core)
    following = ((ctx + 1) % 32, fsdp)
    previous = ((ctx + 31) % 32, fsdp)

    barrier = pltpu.get_barrier_semaphore()
    for d in (xp, xm, yp, ym, zp, zm, partner, sibling, previous):
        pl.semaphore_signal(barrier, inc=1, device_id=d, device_id_type=MESH)
    pl.semaphore_wait(barrier, 9)

    def tslice(ref, half):
        return ref.at[pl.ds(half * 256, 256)]

    def tcopy(j, half, way, dest, src=None):
        src = tall.at[j] if src is None else src
        return pltpu.make_async_remote_copy(
            src_ref=tslice(src, half), dst_ref=tslice(tall.at[j], half),
            send_sem=tss.at[j, half, way], recv_sem=trs.at[j, half],
            device_id=dest, device_id_type=MESH)

    def twait(j, half):
        tcopy(j, half, 0, xp).wait_recv()

    me_t = lo * 4 + x
    sent_sign = 3 - 2 * lo
    cols = [lo, lo + 1 - 2 * (lo % 2), 2 - lo // 2, 3 - 3 * (lo // 2)]
    middle = (lo == 1) | (lo == 2)

    def own_y(start):
        @pl.when(lo < 3)
        def _():
            for half in range(2):
                c = tcopy(me_t, half, 2, yp, tok)
                c.start() if start else c.wait_send()

        @pl.when(lo > 0)
        def _():
            for half in range(2):
                c = tcopy(me_t, half, 3, ym, tok)
                c.start() if start else c.wait_send()

    def along_x(n, half, start):
        j = cols[n] * 4 + x
        src = tok if n == 0 else None
        for way, dest in ((0, xp), (1, xm)):
            c = tcopy(j, half, way, dest, src)
            c.start() if start else c.wait_send()

    def forward_y(n, half, start):
        j = cols[n] * 4 + x
        sign = sent_sign if n == 1 else -sent_sign

        @pl.when(middle)
        def _():
            dest = at(x, lo + sign, hi, z, core)
            c = tcopy(j, half, 2, dest)
            c.start() if start else c.wait_send()

    def forward_x(n, half, start):
        if half == 0:
            c = tcopy(cols[n] * 4 + (x + 3) % 4, 0, 0, xp)
        else:
            c = tcopy(cols[n] * 4 + (x + 1) % 4, 1, 1, xm)
        c.start() if start else c.wait_send()

    def wfull(i):
        return wall.at[i // 2, pl.ds(pl.multiple_of((i % 2) * 256, 256), 256)]

    def wslice(i, half):
        return wall.at[i // 2, pl.ds(pl.multiple_of((i % 2) * 256 + half * 128, 128), 128)]

    def wcopy(i, half, way, dest):
        return pltpu.make_async_remote_copy(
            src_ref=wslice(i, half), dst_ref=wslice(i, half),
            send_sem=wss.at[i, half, way], recv_sem=wrs.at[i, half],
            device_id=dest, device_id_type=MESH)

    def wsib(i):
        return pltpu.make_async_remote_copy(
            src_ref=wfull(i), dst_ref=wfull(i), send_sem=wss.at[i, 0, 2], recv_sem=wrs.at[i, 0],
            device_id=sibling, device_id_type=MESH)

    def wid(stream, distance):
        hh = hi if stream == 0 else 1 - hi
        return (((z + 8 + distance) % 8) * 2 + hh) * 2 + core

    def along_z(stream, k, start):
        for half in range(2):
            if k <= 2 or half == 0:
                c = wcopy(wid(stream, -k), half, 0, zp)
                c.start() if start else c.wait_send()
            if k <= 2 or half == 1:
                c = wcopy(wid(stream, k), half, 1, zm)
                c.start() if start else c.wait_send()

    def z_arrived(stream, k):
        for half in range(2):
            if k < 4 or half == 0:
                wcopy(wid(stream, -k), half, 0, zp).wait_recv()
            if k < 4 or half == 1:
                wcopy(wid(stream, k), half, 1, zm).wait_recv()

    def to_sibling(stream, k, start):
        for distance in sorted({-k, k}) if k < 4 else (4,):
            c = wsib(wid(stream, distance))
            c.start() if start else c.wait_send()

    local = pltpu.make_async_copy(tok, tall.at[me_t], lsem)
    local.start()
    own_y(True)
    for half in range(2):
        along_x(0, half, True)
    for b in range(3):
        wall[ctx // 2, pl.ds(pl.multiple_of(core * 256, 256), 256), b * 256:(b + 1) * 256] = w[:, b, :]
    along_z(0, 0, True)
    to_sibling(0, 0, True)
    for half in range(2):
        wcopy(ctx, half, 3, partner).start()

    def w_step(stream, k):
        z_arrived(stream, k)
        if k < 4:
            along_z(stream, k, True)
        to_sibling(stream, k, True)

    def y_step(n):
        for half in range(2):
            twait(cols[n] * 4 + x, half)
            forward_y(n, half, True)
            along_x(n, half, True)

    def x_step(n):
        twait(cols[n] * 4 + (x + 3) % 4, 0)
        forward_x(n, 0, True)
        twait(cols[n] * 4 + (x + 1) % 4, 1)
        forward_x(n, 1, True)

    w_step(0, 1)
    x_step(0)
    y_step(1)
    w_step(0, 2)
    y_step(2)
    w_step(0, 3)
    x_step(1)
    w_step(0, 4)
    for half in range(2):
        wcopy(wid(1, 0), half, 3, partner).wait_recv()
    along_z(1, 0, True)
    to_sibling(1, 0, True)
    y_step(3)
    w_step(1, 1)
    x_step(2)
    w_step(1, 2)
    w_step(1, 3)
    w_step(1, 4)
    x_step(3)
    for n in range(4):
        twait(cols[n] * 4 + (x + 3) % 4, 1)
        twait(cols[n] * 4 + (x + 1) % 4, 0)
        twait(cols[n] * 4 + (x + 2) % 4, 0)
        twait(cols[n] * 4 + (x + 2) % 4, 1)

    def sib_wait(m, carry):
        i = m * 2 + 1 - core
        wsib(i).wait_recv()
        return carry

    lax.fori_loop(0, 16, sib_wait, 0)
    local.wait()

    acc[...] = jnp.zeros_like(acc)
    ssq[...] = jnp.zeros_like(ssq)

    def chunk(j, carry):
        raw = tall[j].astype(F32)
        sq = raw * raw
        ssq[...] += (sq[:, 0:128] + sq[:, 128:256]) + (sq[:, 256:384] + sq[:, 384:512])
        scaled = (raw * gain[pl.ds(j, 1), :]).astype(BF16)
        acc[...] += jnp.dot(scaled, wall[j], preferred_element_type=F32)
        return carry

    lax.fori_loop(0, 16, chunk, 0)

    scale = lax.rsqrt(jnp.sum(ssq[...], axis=1, keepdims=True) * (1.0 / 8192) + 1e-6)
    projected = (acc[...] * scale).astype(BF16)
    psend[...] = projected[496:512]
    pf[8:520, :] = projected.astype(F32)

    def mixed(start, count, b):
        total = None
        for s in range(SHORT):
            term = sfilt[s, b:b + 1, :] * pf[8 + start - s:8 + start - s + count, b * 256:(b + 1) * 256]
            total = term if total is None else total + term
        return total

    tail = (mixed(384, 128, 1) * mixed(384, 128, 2)).astype(BF16)
    gsend[...] = tail

    def halo(k):
        src, dst = ((gsend, grecv), (psend, precv))[k]
        return pltpu.make_async_remote_copy(
            src_ref=src, dst_ref=dst, send_sem=hss.at[k], recv_sem=hrs.at[k],
            device_id=following, device_id_type=MESH)

    @pl.when(ctx < 31)
    def _():
        halo(0).start()
        halo(1).start()

    @pl.when(ctx > 0)
    def _():
        halo(0).wait_recv()
        halo(1).wait_recv()

    @pl.when(ctx == 0)
    def _():
        grecv[...] = jnp.zeros_like(grecv)
        precv[...] = jnp.zeros_like(precv)

    pf[0:8, :] = precv[8:16, :].astype(F32)
    gext[8:136, :] = grecv[...].astype(F32)
    gext[136:648, :] = (mixed(0, 512, 1) * mixed(0, 512, 2)).astype(BF16).astype(F32)
    query = mixed(0, 512, 0)
    acc[:, 0:256] = query

    for b in range(8):
        gsh[b] = gext[8 - b:648 - b, :]

    def conv(step, carry):
        row = pl.multiple_of((step // 2) * 64, 64)
        lanes = pl.ds(pl.multiple_of((step % 2) * 128, 128), 128)
        total = jnp.zeros((64, 128), F32)
        for b in range(8):
            window = gsh[b, pl.ds(row + 8, 184), lanes]
            for a in range(16):
                total = total + lfilt[8 * a + b:8 * a + b + 1, lanes] * window[8 * (15 - a):8 * (15 - a) + 64]
        out[pl.ds(row, 64), lanes] = (acc[pl.ds(row, 64), lanes] * total).astype(BF16)
        return carry

    lax.fori_loop(0, 16, conv, 0)

    own_y(False)
    for n in range(4):
        for half in range(2):
            along_x(n, half, False)
            forward_x(n, half, False)
            if n > 0:
                forward_y(n, half, False)
    for stream in range(2):
        for k in range(5):
            if k < 4:
                along_z_wait(along_z, stream, k)
            to_sibling(stream, k, False)
    for half in range(2):
        wcopy(ctx, half, 3, partner).wait_send()

    @pl.when(ctx < 31)
    def _():
        halo(0).wait_send()
        halo(1).wait_send()


def along_z_wait(along_z, stream, k):
    along_z(stream, k, False)


def on_device(tokens, gain, in_weight, short_filter, long_filter):
    vmem = pl.BlockSpec(memory_space=pltpu.VMEM)
    dma = pltpu.SemaphoreType.DMA
    return pl.pallas_call(
        kernel,
        out_shape=jax.ShapeDtypeStruct((ROWS, CHAN), BF16),
        in_specs=[pl.BlockSpec(memory_space=pl.ANY), vmem, vmem, vmem, vmem],
        out_specs=vmem,
        scratch_shapes=[
            pltpu.VMEM((16, ROWS, FEATS), BF16),
            pltpu.VMEM((16, 512, 3 * CHAN), BF16),
            pltpu.VMEM((ROWS, 3 * CHAN), F32),
            pltpu.VMEM((ROWS, 128), F32),
            pltpu.VMEM((ROWS + 8, 3 * CHAN), F32),
            pltpu.VMEM((ROWS + 136, CHAN), F32),
            pltpu.VMEM((8, ROWS + 128, CHAN), F32),
            pltpu.VMEM((128, CHAN), BF16),
            pltpu.VMEM((16, 3 * CHAN), BF16),
            pltpu.VMEM((128, CHAN), BF16),
            pltpu.VMEM((16, 3 * CHAN), BF16),
            dma,
            dma((16, 2, 4)),
            dma((16, 2)),
            dma((32, 2, 4)),
            dma((32, 2)),
            dma((2,)),
            dma((2,)),
        ],
        name="hyena",
        compiler_params=pltpu.CompilerParams(
            collective_id=0, has_side_effects=True, vmem_limit_bytes=56 << 20),
    )(tokens, gain.reshape(16, 512), in_weight, short_filter, long_filter)


def solution(mesh):
    return jax.shard_map(
        on_device,
        mesh=mesh,
        in_specs=(
            P("ctx", "fsdp"),
            P(),
            P("ctx", None, "fsdp"),
            P(None, None, "fsdp"),
            P(None, "fsdp"),
        ),
        out_specs=P("ctx", "fsdp"),
        check_vma=False,
    )
```

time: 361 us -> 134 us (0.37); the launches traced: 354 us -> 133 us
  waiting for transfers between devices: 285 us -> 0 us
  Pallas kernels: 0 us -> 128 us
  other arithmetic: 19.3 us -> 0 us
  between operations: 13.5 us -> 0.01 us
  matrix products: 13.1 us -> 0 us
  starting transfers between devices: 9.65 us -> 0 us
  local copies, waits for them, and re-layouts: 10.6 us -> 5.17 us
    all_gather x2 -> x0, waiting for transfers between devices: 282 us -> none  [the longest x1 172 us: on_device(): panel_rows = lax.all_gather(in_weight, 'ctx', axis=0, tiled=True)]
    pallas_call x0 -> x1, Pallas kernels: none -> 128 us  [on_device(): pl.pallas_call(kernel, out_shape=jax.ShapeDtypeStruct((ROWS, CHAN), BF16)...]
    add x9 -> x0, other arithmetic: 13.1 us -> none  [the longest x8 12.7 us: group_step(): accumulated = accumulated + tap_weights * window_rows]
    dot_general x1 -> x0, matrix products: 13.1 us -> none  [on_device(): jnp.dot(normed, panel_rows.reshape(panel_rows.shape[0], 3 * channels), pr...]
    ppermute x2 -> x0, starting transfers between devices: 9.61 us -> none  [passed_along(): lax.ppermute(value, axis, [(source, source + steps) for source in range(l...]
    dynamic_slice x8 -> x0, local copies, waits for them, and re-layouts: 8.62 us -> none  [group_step(): tap_weights = lax.dynamic_slice_in_dim(filters, lag_value, 1, 0)]
    reduce_sum x1 -> x0, other arithmetic: 5.1 us -> none  [on_device(): mean_square = jnp.mean(widened * widened, axis=1, keepdims=True)]
  transfers between devices with their start and end apart: 4 -> 0, of which waited for: 4 -> 0; matrix products, arithmetic and copies ran while one was open for 2% -> 0% of each run, Pallas kernels for 0% -> 0%
where the time goes in v1:
time: 134 us; the launch traced here: 133 us
  Pallas kernels  128 us (96%)
  local copies, waits for them, and re-layouts  5.17 us (4%)
    pallas_call x1, Pallas kernels, on_device(): pl.pallas_call(kernel, out_shape=jax.ShapeDtypeStruct((ROWS, CHAN), BF16)...  128 us
    unnamed x2, local copies, waits for them, and re-layouts  3.79 us

profile of v1, /device:TPU:1, one launch (start us, length us, event | category | flops | bytes accessed | tf_op | source)
XLA Modules:
  0.0 133.5 jit_solution(17991003593301328992)
XLA Ops:
  0.0 1.4 %reshape.3.gain = f32[16,512]{1,0:T(8,128)} reshape(f32[8192]{0:T(1024)} %param.6) | data formatting | bytes 65536 | tf_op jit(solution)/shard_map/reshape | solution.py:331
  1.4 2.1 %copy.6.w = bf16[256,3,256]{2,1,0:T(4,128)(2,1)} copy(bf16[256,3,256]{2,0,1:T(8,128)(2,1)} %param.7) | data formatting | bytes 786432 | tf_op args[2]
  3.5 128.3 %hyena.1 = bf16[512,256]{1,0:T(8,128)(2,1)} custom-call(bf16[512,512]{1,0:T(8,128)(2,1)} %tok.1, f32[16,512]{1,0:T(8,128)} %reshape.3.gain, bf16[256,3,256]{2,1,0:T(4,128)(2,1)} %copy.6.w, f32[3,3,256]{2,1,0:T(4,128)} %sfilt.1, f32[128,256]{1,0:T(8,128)} %lfilt.1), custom_call_target="tpu_custom_call" | custom-call | tf_op jit(solution)/shard_map/hyena/pallas_call | solution.py:303
  131.8 1.7 %copy.8 = bf16[512,256]{1,0:T(8,128)(2,1)} copy(bf16[512,256]{1,0:T(8,128)(2,1)} %hyena.1) | data formatting | bytes 524288

commit v2 on v1

--- a/solution.py
+++ b/solution.py
@@ -59,18 +59,16 @@
     cols = [lo, lo + 1 - 2 * (lo % 2), 2 - lo // 2, 3 - 3 * (lo // 2)]
     middle = (lo == 1) | (lo == 2)
 
-    def own_y(start):
+    def own_y(half, start):
         @pl.when(lo < 3)
         def _():
-            for half in range(2):
-                c = tcopy(me_t, half, 2, yp, tok)
-                c.start() if start else c.wait_send()
+            c = tcopy(me_t, half, 2, yp, tok)
+            c.start() if start else c.wait_send()
 
         @pl.when(lo > 0)
         def _():
-            for half in range(2):
-                c = tcopy(me_t, half, 3, ym, tok)
-                c.start() if start else c.wait_send()
+            c = tcopy(me_t, half, 3, ym, tok)
+            c.start() if start else c.wait_send()
 
     def along_x(n, half, start):
         j = cols[n] * 4 + x
@@ -96,123 +94,167 @@
             c = tcopy(cols[n] * 4 + (x + 1) % 4, 1, 1, xm)
         c.start() if start else c.wait_send()
 
+    def wpart(i, half):
+        return wall.at[i // 2, :, pl.ds(pl.multiple_of((i % 2) * 256 + half * 128, 128), 128)]
+
     def wfull(i):
-        return wall.at[i // 2, pl.ds(pl.multiple_of((i % 2) * 256, 256), 256)]
-
-    def wslice(i, half):
-        return wall.at[i // 2, pl.ds(pl.multiple_of((i % 2) * 256 + half * 128, 128), 128)]
-
-    def wcopy(i, half, way, dest):
+        return wall.at[i // 2, :, pl.ds(pl.multiple_of((i % 2) * 256, 256), 256)]
+
+    def wcopy(i, half, way, dest, own=False):
         return pltpu.make_async_remote_copy(
-            src_ref=wslice(i, half), dst_ref=wslice(i, half),
+            src_ref=w.at[:, pl.ds(half * 128, 128)] if own else wpart(i, half), dst_ref=wpart(i, half),
             send_sem=wss.at[i, half, way], recv_sem=wrs.at[i, half],
             device_id=dest, device_id_type=MESH)
 
-    def wsib(i):
+    def wsib(i, own=False):
         return pltpu.make_async_remote_copy(
-            src_ref=wfull(i), dst_ref=wfull(i), send_sem=wss.at[i, 0, 2], recv_sem=wrs.at[i, 0],
+            src_ref=w if own else wfull(i), dst_ref=wfull(i), send_sem=wss.at[i, 0, 2], recv_sem=wrs.at[i, 0],
             device_id=sibling, device_id_type=MESH)
 
     def wid(stream, distance):
         hh = hi if stream == 0 else 1 - hi
         return (((z + 8 + distance) % 8) * 2 + hh) * 2 + core
 
-    def along_z(stream, k, start):
-        for half in range(2):
-            if k <= 2 or half == 0:
-                c = wcopy(wid(stream, -k), half, 0, zp)
-                c.start() if start else c.wait_send()
-            if k <= 2 or half == 1:
-                c = wcopy(wid(stream, k), half, 1, zm)
-                c.start() if start else c.wait_send()
-
-    def z_arrived(stream, k):
-        for half in range(2):
-            if k < 4 or half == 0:
-                wcopy(wid(stream, -k), half, 0, zp).wait_recv()
-            if k < 4 or half == 1:
-                wcopy(wid(stream, k), half, 1, zm).wait_recv()
+    def along_z(stream, k, half, start):
+        own = stream == 0 and k == 0
+        if k <= 2 or half == 0:
+            c = wcopy(wid(stream, -k), half, 0, zp, own)
+            c.start() if start else c.wait_send()
+        if k <= 2 or half == 1:
+            c = wcopy(wid(stream, k), half, 1, zm, own)
+            c.start() if start else c.wait_send()
 
     def to_sibling(stream, k, start):
         for distance in sorted({-k, k}) if k < 4 else (4,):
-            c = wsib(wid(stream, distance))
-            c.start() if start else c.wait_send()
-
-    local = pltpu.make_async_copy(tok, tall.at[me_t], lsem)
-    local.start()
-    own_y(True)
-    for half in range(2):
-        along_x(0, half, True)
-    for b in range(3):
-        wall[ctx // 2, pl.ds(pl.multiple_of(core * 256, 256), 256), b * 256:(b + 1) * 256] = w[:, b, :]
-    along_z(0, 0, True)
-    to_sibling(0, 0, True)
-    for half in range(2):
-        wcopy(ctx, half, 3, partner).start()
-
-    def w_step(stream, k):
-        z_arrived(stream, k)
-        if k < 4:
-            along_z(stream, k, True)
-        to_sibling(stream, k, True)
-
-    def y_step(n):
-        for half in range(2):
-            twait(cols[n] * 4 + x, half)
-            forward_y(n, half, True)
-            along_x(n, half, True)
-
-    def x_step(n):
-        twait(cols[n] * 4 + (x + 3) % 4, 0)
-        forward_x(n, 0, True)
-        twait(cols[n] * 4 + (x + 1) % 4, 1)
-        forward_x(n, 1, True)
-
-    w_step(0, 1)
-    x_step(0)
-    y_step(1)
-    w_step(0, 2)
-    y_step(2)
-    w_step(0, 3)
-    x_step(1)
-    w_step(0, 4)
-    for half in range(2):
+            c = wsib(wid(stream, distance), stream == 0 and k == 0)
+            c.start() if start else c.wait_send()
+
+    def to_partner(half, start):
+        c = wcopy(ctx, half, 3, partner, True)
+        c.start() if start else c.wait_send()
+
+    local_t = pltpu.make_async_copy(tok, tall.at[me_t], lsem.at[0])
+    local_w = pltpu.make_async_copy(w, wfull(ctx), lsem.at[1])
+
+    def w_step(stream, k, half):
+        if k < 4 or half == 0:
+            wcopy(wid(stream, -k), half, 0, zp).wait_recv()
+            if k <= 2 or (k == 3 and half == 0):
+                wcopy(wid(stream, -k), half, 0, zp).start()
+        if k < 4 or half == 1:
+            wcopy(wid(stream, k), half, 1, zm).wait_recv()
+            if k <= 2 or (k == 3 and half == 1):
+                wcopy(wid(stream, k), half, 1, zm).start()
+        if half == 1:
+            to_sibling(stream, k, True)
+
+    def p_step(half):
         wcopy(wid(1, 0), half, 3, partner).wait_recv()
-    along_z(1, 0, True)
-    to_sibling(1, 0, True)
-    y_step(3)
-    w_step(1, 1)
-    x_step(2)
-    w_step(1, 2)
-    w_step(1, 3)
-    w_step(1, 4)
-    x_step(3)
-    for n in range(4):
+        along_z(1, 0, half, True)
+        if half == 1:
+            to_sibling(1, 0, True)
+
+    def y_step(n, half):
+        twait(cols[n] * 4 + x, half)
+        forward_y(n, half, True)
+        along_x(n, half, True)
+
+    def x_step(n, half):
+        twait(cols[n] * 4 + ((x + 3) % 4 if half == 0 else (x + 1) % 4), half)
+        forward_x(n, half, True)
+
+    def column_done(n):
         twait(cols[n] * 4 + (x + 3) % 4, 1)
         twait(cols[n] * 4 + (x + 1) % 4, 0)
         twait(cols[n] * 4 + (x + 2) % 4, 0)
         twait(cols[n] * 4 + (x + 2) % 4, 1)
 
-    def sib_wait(m, carry):
-        i = m * 2 + 1 - core
-        wsib(i).wait_recv()
-        return carry
-
-    lax.fori_loop(0, 16, sib_wait, 0)
-    local.wait()
-
-    acc[...] = jnp.zeros_like(acc)
-    ssq[...] = jnp.zeros_like(ssq)
-
-    def chunk(j, carry):
+    def siblings_done(stream):
+        hh = hi if stream == 0 else 1 - hi
+
+        def one(m, carry):
+            wsib((m * 2 + hh) * 2 + 1 - core).wait_recv()
+            return carry
+
+        lax.fori_loop(0, 8, one, 0)
+
+    def chunk(j):
         raw = tall[j].astype(F32)
         sq = raw * raw
         ssq[...] += (sq[:, 0:128] + sq[:, 128:256]) + (sq[:, 256:384] + sq[:, 384:512])
-        scaled = (raw * gain[pl.ds(j, 1), :]).astype(BF16)
-        acc[...] += jnp.dot(scaled, wall[j], preferred_element_type=F32)
-        return carry
-
-    lax.fori_loop(0, 16, chunk, 0)
+        scaled = (raw * gain[:, pl.ds(pl.multiple_of(j * 512, 512), 512)]).astype(BF16)
+        for b in range(3):
+            acc[:, b * 256:(b + 1) * 256] += jnp.dot(scaled, wall[j, b], preferred_element_type=F32)
+
+    def products(n, stream):
+        hh = hi if stream == 0 else 1 - hi
+
+        def one(m, carry):
+            chunk(cols[n] * 4 + hh + 2 * m)
+            return carry
+
+        lax.fori_loop(0, 2, one, 0)
+
+    for half in range(2):
+        along_z(0, 0, half, True)
+        along_x(0, half, True)
+        own_y(half, True)
+    to_sibling(0, 0, True)
+    local_t.start()
+    local_w.start()
+    acc[...] = jnp.zeros_like(acc)
+    ssq[...] = jnp.zeros_like(ssq)
+
+    w_step(0, 1, 0)
+    x_step(0, 0)
+    y_step(1, 0)
+    w_step(0, 1, 1)
+    w_step(0, 2, 0)
+    x_step(0, 1)
+    y_step(1, 1)
+    to_partner(0, True)
+    w_step(0, 2, 1)
+    y_step(2, 0)
+    w_step(0, 3, 0)
+    y_step(2, 1)
+    to_partner(1, True)
+    x_step(1, 0)
+    w_step(0, 3, 1)
+    x_step(1, 1)
+    w_step(0, 4, 0)
+    w_step(0, 4, 1)
+    local_t.wait()
+    local_w.wait()
+    column_done(0)
+    siblings_done(0)
+    products(0, 0)
+    p_step(0)
+    y_step(3, 0)
+    p_step(1)
+    column_done(1)
+    products(1, 0)
+    w_step(1, 1, 0)
+    y_step(3, 1)
+    w_step(1, 1, 1)
+    x_step(2, 0)
+    w_step(1, 2, 0)
+    x_step(2, 1)
+    w_step(1, 2, 1)
+    column_done(2)
+    products(2, 0)
+    w_step(1, 3, 0)
+    w_step(1, 3, 1)
+    x_step(3, 0)
+    w_step(1, 4, 0)
+    w_step(1, 4, 1)
+    siblings_done(1)
+    products(0, 1)
+    products(1, 1)
+    x_step(3, 1)
+    products(2, 1)
+    column_done(3)
+    products(3, 0)
+    products(3, 1)
 
     scale = lax.rsqrt(jnp.sum(ssq[...], axis=1, keepdims=True) * (1.0 / 8192) + 1e-6)
     projected = (acc[...] * scale).astype(BF16)
@@ -272,20 +314,20 @@
 
     lax.fori_loop(0, 16, conv, 0)
 
-    own_y(False)
-    for n in range(4):
-        for half in range(2):
+    for half in range(2):
+        own_y(half, False)
+        to_partner(half, False)
+        for n in range(4):
             along_x(n, half, False)
             forward_x(n, half, False)
             if n > 0:
                 forward_y(n, half, False)
+        for stream in range(2):
+            for k in range(4):
+                along_z(stream, k, half, False)
     for stream in range(2):
         for k in range(5):
-            if k < 4:
-                along_z_wait(along_z, stream, k)
             to_sibling(stream, k, False)
-    for half in range(2):
-        wcopy(ctx, half, 3, partner).wait_send()
 
     @pl.when(ctx < 31)
     def _():
@@ -293,21 +335,18 @@
         halo(1).wait_send()
 
 
-def along_z_wait(along_z, stream, k):
-    along_z(stream, k, False)
-
-
 def on_device(tokens, gain, in_weight, short_filter, long_filter):
     vmem = pl.BlockSpec(memory_space=pltpu.VMEM)
+    anywhere = pl.BlockSpec(memory_space=pl.ANY)
     dma = pltpu.SemaphoreType.DMA
     return pl.pallas_call(
         kernel,
         out_shape=jax.ShapeDtypeStruct((ROWS, CHAN), BF16),
-        in_specs=[pl.BlockSpec(memory_space=pl.ANY), vmem, vmem, vmem, vmem],
+        in_specs=[anywhere, vmem, anywhere, vmem, vmem],
         out_specs=vmem,
         scratch_shapes=[
             pltpu.VMEM((16, ROWS, FEATS), BF16),
-            pltpu.VMEM((16, 512, 3 * CHAN), BF16),
+            pltpu.VMEM((16, 3, 512, CHAN), BF16),
             pltpu.VMEM((ROWS, 3 * CHAN), F32),
             pltpu.VMEM((ROWS, 128), F32),
             pltpu.VMEM((ROWS + 8, 3 * CHAN), F32),
@@ -317,7 +356,7 @@
             pltpu.VMEM((16, 3 * CHAN), BF16),
             pltpu.VMEM((128, CHAN), BF16),
             pltpu.VMEM((16, 3 * CHAN), BF16),
-            dma,
+            dma((2,)),
             dma((16, 2, 4)),
             dma((16, 2)),
             dma((32, 2, 4)),
@@ -328,7 +367,7 @@
         name="hyena",
         compiler_params=pltpu.CompilerParams(
             collective_id=0, has_side_effects=True, vmem_limit_bytes=56 << 20),
-    )(tokens, gain.reshape(16, 512), in_weight, short_filter, long_filter)
+    )(tokens, gain.reshape(1, 8192), in_weight.transpose(1, 0, 2), short_filter, long_filter)
 
 
 def solution(mesh):

time: 134 us -> 126 us (0.940)
  Pallas kernels: 128 us -> 123 us
  local copies, waits for them, and re-layouts: 5.17 us -> 1.67 us
    pallas_call x1, Pallas kernels: 128 us -> 123 us  [on_device(): pl.pallas_call(kernel, out_shape=jax.ShapeDtypeStruct((ROWS, CHAN), BF16)...]
    unnamed x2 -> x1, local copies, waits for them, and re-layouts: 3.79 us -> 1.67 us
    reshape x1 -> x0, local copies, waits for them, and re-layouts: 1.38 us -> none  [on_device(): gain.reshape(16, 512)]
where the time goes in v2:
time: 126 us; the launch traced here: 125 us
  Pallas kernels  123 us (98%)
  local copies, waits for them, and re-layouts  1.67 us (1%)
    pallas_call x1, Pallas kernels, on_device(): pl.pallas_call(kernel, out_shape=jax.ShapeDtypeStruct((ROWS, CHAN), BF16)...  123 us

profile of v2, /device:TPU:1, one launch (start us, length us, event | category | flops | bytes accessed | tf_op | source)
XLA Modules:
  0.0 124.8 jit_solution(5226801845122179063)
XLA Ops:
  0.0 123.1 %hyena.1 = bf16[512,256]{1,0:T(8,128)(2,1)} custom-call(bf16[512,512]{1,0:T(8,128)(2,1)} %tok.1, f32[1,8192]{1,0:T(1,128)} %bitcast.3, bf16[3,256,256]{2,1,0:T(8,128)(2,1)} %bitcast.2, f32[3,3,256]{2,1,0:T(4,128)} %sfilt.1, f32[128,256]{1,0:T(8,128)} %lfilt.1), custom_call_target="tpu_custom_call" | custom-call | tf_op jit(solution)/shard_map/hyena/pallas_call | solution.py:342
  123.1 1.7 %copy.7 = bf16[512,256]{1,0:T(8,128)(2,1)} copy(bf16[512,256]{1,0:T(8,128)(2,1)} %hyena.1) | data formatting | bytes 524288

commit v3 on v2

--- a/solution.py
+++ b/solution.py
@@ -13,7 +13,29 @@
 TAPS, SHORT = 128, 3
 
 
-def kernel(tok, gain, w, sfilt, lfilt, out, tall, wall, acc, ssq, pf, gext, gsh, gsend, psend, grecv, precv,
+def split_taps(values):
+    pairs = values.reshape(values.shape[0] // 2, 2, 8, CHAN)
+    even, odd = pairs[:, 0], pairs[:, 1]
+    return [odd, even + odd, even]
+
+
+def split_tiles(tiles, count):
+    def tile(s):
+        return tiles[s + count - 1]
+
+    at = range(1 - count // 2, (len(tiles) - count + 1) // 2)
+    return [[tile(2 * m - 1) - tile(2 * m) for m in at], [tile(2 * m) for m in at],
+            [tile(2 * m + 1) - tile(2 * m) for m in at]]
+
+
+def joined(parts):
+    result = []
+    for before, both, after in zip(*parts):
+        result += [both + before, both + after]
+    return result
+
+
+def kernel(tok, gain, w, sfilt, lfilt, out, tall, wall, acc, ssq, pf, gext, gsh, taps, gsend, psend, grecv, precv,
            lsem, tss, trs, wss, wrs, hss, hrs):
     ctx = lax.axis_index("ctx")
     fsdp = lax.axis_index("fsdp")
@@ -196,14 +218,23 @@
         lax.fori_loop(0, 2, one, 0)
 
     for half in range(2):
+        if half == 1:
+            along_z(0, 0, 0, False)
+            along_x(0, 0, False)
         along_z(0, 0, half, True)
         along_x(0, half, True)
+        if half == 1:
+            own_y(0, False)
         own_y(half, True)
+    to_partner(0, True)
     to_sibling(0, 0, True)
     local_t.start()
     local_w.start()
     acc[...] = jnp.zeros_like(acc)
     ssq[...] = jnp.zeros_like(ssq)
+    for i, outer in enumerate(split_taps(lfilt[...].reshape(16, 8, CHAN))):
+        for j, inner in enumerate(split_taps(outer)):
+            taps[i * 3 + j] = inner
 
     w_step(0, 1, 0)
     x_step(0, 0)
@@ -212,7 +243,6 @@
     w_step(0, 2, 0)
     x_step(0, 1)
     y_step(1, 1)
-    to_partner(0, True)
     w_step(0, 2, 1)
     y_step(2, 0)
     w_step(0, 3, 0)
@@ -302,29 +332,41 @@
         gsh[b] = gext[8 - b:648 - b, :]
 
     def conv(step, carry):
-        row = pl.multiple_of((step // 2) * 64, 64)
+        row = pl.multiple_of((step // 2) * 128, 128)
         lanes = pl.ds(pl.multiple_of((step % 2) * 128, 128), 128)
-        total = jnp.zeros((64, 128), F32)
-        for b in range(8):
-            window = gsh[b, pl.ds(row + 8, 184), lanes]
-            for a in range(16):
-                total = total + lfilt[8 * a + b:8 * a + b + 1, lanes] * window[8 * (15 - a):8 * (15 - a) + 64]
-        out[pl.ds(row, 64), lanes] = (acc[pl.ds(row, 64), lanes] * total).astype(BF16)
+        merged = []
+        for i in range(3):
+            sums = [[None] * 4 for _ in range(3)]
+            for b in range(8):
+                window = gsh[b, pl.ds(row + 8, 248), lanes]
+                tiles = [window[8 * t:8 * t + 8] for t in range(31)]
+                for j, part in enumerate(split_tiles(split_tiles(tiles, 16)[i], 8)):
+                    for c in range(4):
+                        weight = taps[i * 3 + j, c, b:b + 1, lanes]
+                        for m in range(4):
+                            term = weight * part[m + 3 - c]
+                            sums[j][m] = term if sums[j][m] is None else sums[j][m] + term
+            merged.append(joined(sums))
+        response = jnp.concatenate(joined(merged), axis=0)
+        out[pl.ds(row, 128), lanes] = (acc[pl.ds(row, 128), lanes] * response).astype(BF16)
         return carry
 
-    lax.fori_loop(0, 16, conv, 0)
+    lax.fori_loop(0, 8, conv, 0)
 
     for half in range(2):
-        own_y(half, False)
+        if half == 1:
+            own_y(half, False)
         to_partner(half, False)
         for n in range(4):
-            along_x(n, half, False)
+            if n > 0 or half == 1:
+                along_x(n, half, False)
             forward_x(n, half, False)
             if n > 0:
                 forward_y(n, half, False)
         for stream in range(2):
             for k in range(4):
-                along_z(stream, k, half, False)
+                if stream + k + half > 0:
+                    along_z(stream, k, half, False)
     for stream in range(2):
         for k in range(5):
             to_sibling(stream, k, False)
@@ -352,6 +394,7 @@
             pltpu.VMEM((ROWS + 8, 3 * CHAN), F32),
             pltpu.VMEM((ROWS + 136, CHAN), F32),
             pltpu.VMEM((8, ROWS + 128, CHAN), F32),
+            pltpu.VMEM((9, 4, 8, CHAN), F32),
             pltpu.VMEM((128, CHAN), BF16),
             pltpu.VMEM((16, 3 * CHAN), BF16),
             pltpu.VMEM((128, CHAN), BF16),

time: 126 us -> 123 us (0.976)
  Pallas kernels: 123 us -> 120 us
    pallas_call x1, Pallas kernels: 123 us -> 120 us  [on_device(): pl.pallas_call(kernel, out_shape=jax.ShapeDtypeStruct((ROWS, CHAN), BF16)...]
where the time goes in v3:
time: 123 us; the launch traced here: 122 us
  Pallas kernels  120 us (98%)
  local copies, waits for them, and re-layouts  1.67 us (1%)
    pallas_call x1, Pallas kernels, on_device(): pl.pallas_call(kernel, out_shape=jax.ShapeDtypeStruct((ROWS, CHAN), BF16)...  120 us

profile of v3, /device:TPU:1, one launch (start us, length us, event | category | flops | bytes accessed | tf_op | source)
XLA Modules:
  0.0 121.6 jit_solution(6393782799047270863)
XLA Ops:
  0.0 119.9 %hyena.1 = bf16[512,256]{1,0:T(8,128)(2,1)} custom-call(bf16[512,512]{1,0:T(8,128)(2,1)} %tok.1, f32[1,8192]{1,0:T(1,128)} %bitcast.3, bf16[3,256,256]{2,1,0:T(8,128)(2,1)} %bitcast.2, f32[3,3,256]{2,1,0:T(4,128)} %sfilt.1, f32[128,256]{1,0:T(8,128)} %lfilt.1), custom_call_target="tpu_custom_call" | custom-call | tf_op jit(solution)/shard_map/hyena/pallas_call | solution.py:384
  119.9 1.7 %copy.7 = bf16[512,256]{1,0:T(8,128)(2,1)} copy(bf16[512,256]{1,0:T(8,128)(2,1)} %hyena.1) | data formatting | bytes 524288

commit v4 on v3

--- a/solution.py
+++ b/solution.py
@@ -35,7 +35,7 @@
     return result
 
 
-def kernel(tok, gain, w, sfilt, lfilt, out, tall, wall, acc, ssq, pf, gext, gsh, taps, gsend, psend, grecv, precv,
+def kernel(tok, gain, w, sfilt, lfilt, out, tall, scaled, wall, acc, ssq, pf, gext, gsh, taps, gsend, psend, grecv, precv,
            lsem, tss, trs, wss, wrs, hss, hrs):
     ctx = lax.axis_index("ctx")
     fsdp = lax.axis_index("fsdp")
@@ -200,22 +200,24 @@
 
         lax.fori_loop(0, 8, one, 0)
 
-    def chunk(j):
-        raw = tall[j].astype(F32)
-        sq = raw * raw
-        ssq[...] += (sq[:, 0:128] + sq[:, 128:256]) + (sq[:, 256:384] + sq[:, 384:512])
-        scaled = (raw * gain[:, pl.ds(pl.multiple_of(j * 512, 512), 512)]).astype(BF16)
-        for b in range(3):
-            acc[:, b * 256:(b + 1) * 256] += jnp.dot(scaled, wall[j, b], preferred_element_type=F32)
+    def scale_column(n):
+        def one(m, carry):
+            j = cols[n] * 4 + m
+            raw = tall[j].astype(F32)
+            sq = raw * raw
+            ssq[...] += (sq[:, 0:128] + sq[:, 128:256]) + (sq[:, 256:384] + sq[:, 384:512])
+            scaled[j] = (raw * gain[:, pl.ds(pl.multiple_of(j * 512, 512), 512)]).astype(BF16)
+            return carry
+
+        lax.fori_loop(0, 4, one, 0)
 
     def products(n, stream):
         hh = hi if stream == 0 else 1 - hi
-
-        def one(m, carry):
-            chunk(cols[n] * 4 + hh + 2 * m)
-            return carry
-
-        lax.fori_loop(0, 2, one, 0)
+        first = cols[n] * 4 + hh
+        for b in range(3):
+            acc[:, b * 256:(b + 1) * 256] += (
+                jnp.dot(scaled[first], wall[first, b], preferred_element_type=F32)
+                + jnp.dot(scaled[first + 2], wall[first + 2, b], preferred_element_type=F32))
 
     for half in range(2):
         if half == 1:
@@ -240,49 +242,53 @@
     x_step(0, 0)
     y_step(1, 0)
     w_step(0, 1, 1)
-    w_step(0, 2, 0)
     x_step(0, 1)
     y_step(1, 1)
+    w_step(0, 2, 0)
+    y_step(2, 0)
     w_step(0, 2, 1)
-    y_step(2, 0)
     w_step(0, 3, 0)
+    x_step(1, 0)
     y_step(2, 1)
-    to_partner(1, True)
-    x_step(1, 0)
     w_step(0, 3, 1)
     x_step(1, 1)
+    to_partner(1, True)
+    p_step(0)
     w_step(0, 4, 0)
     w_step(0, 4, 1)
     local_t.wait()
     local_w.wait()
     column_done(0)
+    scale_column(0)
     siblings_done(0)
     products(0, 0)
-    p_step(0)
     y_step(3, 0)
     p_step(1)
     column_done(1)
+    scale_column(1)
     products(1, 0)
     w_step(1, 1, 0)
     y_step(3, 1)
+    x_step(2, 0)
     w_step(1, 1, 1)
-    x_step(2, 0)
     w_step(1, 2, 0)
     x_step(2, 1)
     w_step(1, 2, 1)
     column_done(2)
+    scale_column(2)
     products(2, 0)
     w_step(1, 3, 0)
     w_step(1, 3, 1)
     x_step(3, 0)
+    x_step(3, 1)
     w_step(1, 4, 0)
     w_step(1, 4, 1)
     siblings_done(1)
     products(0, 1)
     products(1, 1)
-    x_step(3, 1)
     products(2, 1)
     column_done(3)
+    scale_column(3)
     products(3, 0)
     products(3, 1)
 
@@ -312,24 +318,13 @@
         halo(0).start()
         halo(1).start()
 
-    @pl.when(ctx > 0)
-    def _():
-        halo(0).wait_recv()
-        halo(1).wait_recv()
-
-    @pl.when(ctx == 0)
-    def _():
-        grecv[...] = jnp.zeros_like(grecv)
-        precv[...] = jnp.zeros_like(precv)
-
-    pf[0:8, :] = precv[8:16, :].astype(F32)
-    gext[8:136, :] = grecv[...].astype(F32)
-    gext[136:648, :] = (mixed(0, 512, 1) * mixed(0, 512, 2)).astype(BF16).astype(F32)
-    query = mixed(0, 512, 0)
-    acc[:, 0:256] = query
-
+    def gate(start, count):
+        return (mixed(start, count, 1) * mixed(start, count, 2)).astype(BF16).astype(F32)
+
+    gext[144:648, :] = gate(8, 504)
+    acc[8:512, 0:256] = mixed(8, 504, 0)
     for b in range(8):
-        gsh[b] = gext[8 - b:648 - b, :]
+        gsh[b, 144:640] = gext[152 - b:648 - b, :]
 
     def conv(step, carry):
         row = pl.multiple_of((step // 2) * 128, 128)
@@ -351,7 +346,26 @@
         out[pl.ds(row, 128), lanes] = (acc[pl.ds(row, 128), lanes] * response).astype(BF16)
         return carry
 
-    lax.fori_loop(0, 8, conv, 0)
+    lax.fori_loop(4, 8, conv, 0)
+
+    @pl.when(ctx > 0)
+    def _():
+        halo(0).wait_recv()
+        halo(1).wait_recv()
+
+    @pl.when(ctx == 0)
+    def _():
+        grecv[...] = jnp.zeros_like(grecv)
+        precv[...] = jnp.zeros_like(precv)
+
+    pf[0:8, :] = precv[8:16, :].astype(F32)
+    gext[8:136, :] = grecv[...].astype(F32)
+    gext[136:144, :] = gate(0, 8)
+    acc[0:8, 0:256] = mixed(0, 8, 0)
+    for b in range(8):
+        gsh[b, 0:144] = gext[8 - b:152 - b, :]
+
+    lax.fori_loop(0, 4, conv, 0)
 
     for half in range(2):
         if half == 1:
@@ -387,6 +401,7 @@
         in_specs=[anywhere, vmem, anywhere, vmem, vmem],
         out_specs=vmem,
         scratch_shapes=[
+            pltpu.VMEM((16, ROWS, FEATS), BF16),
             pltpu.VMEM((16, ROWS, FEATS), BF16),
             pltpu.VMEM((16, 3, 512, CHAN), BF16),
             pltpu.VMEM((ROWS, 3 * CHAN), F32),

time: 123 us -> 114 us (0.927)
  Pallas kernels: 120 us -> 112 us
    pallas_call x1, Pallas kernels: 120 us -> 112 us  [on_device(): pl.pallas_call(kernel, out_shape=jax.ShapeDtypeStruct((ROWS, CHAN), BF16)...]
where the time goes in v4:
time: 114 us
  Pallas kernels  112 us (98%)
  local copies, waits for them, and re-layouts  1.67 us (1%)
    pallas_call x1, Pallas kernels, on_device(): pl.pallas_call(kernel, out_shape=jax.ShapeDtypeStruct((ROWS, CHAN), BF16)...  112 us

profile of v4, /device:TPU:1, one launch (start us, length us, event | category | flops | bytes accessed | tf_op | source)
XLA Modules:
  0.0 113.8 jit_solution(8760235805731637926)
XLA Ops:
  0.0 112.1 %hyena.1 = bf16[512,256]{1,0:T(8,128)(2,1)} custom-call(bf16[512,512]{1,0:T(8,128)(2,1)} %tok.1, f32[1,8192]{1,0:T(1,128)} %bitcast.3, bf16[3,256,256]{2,1,0:T(8,128)(2,1)} %bitcast.2, f32[3,3,256]{2,1,0:T(4,128)} %sfilt.1, f32[128,256]{1,0:T(8,128)} %lfilt.1), custom_call_target="tpu_custom_call" | custom-call | tf_op jit(solution)/shard_map/hyena/pallas_call | solution.py:398
  112.1 1.7 %copy.7 = bf16[512,256]{1,0:T(8,128)(2,1)} copy(bf16[512,256]{1,0:T(8,128)(2,1)} %hyena.1) | data formatting | bytes 524288

commit v5 on v4

--- a/solution.py
+++ b/solution.py
@@ -256,31 +256,31 @@
     p_step(0)
     w_step(0, 4, 0)
     w_step(0, 4, 1)
+    y_step(3, 0)
+    p_step(1)
+    w_step(1, 1, 0)
+    y_step(3, 1)
+    x_step(2, 0)
     local_t.wait()
     local_w.wait()
     column_done(0)
     scale_column(0)
     siblings_done(0)
     products(0, 0)
-    y_step(3, 0)
-    p_step(1)
+    w_step(1, 1, 1)
+    w_step(1, 2, 0)
     column_done(1)
     scale_column(1)
+    x_step(2, 1)
     products(1, 0)
-    w_step(1, 1, 0)
-    y_step(3, 1)
-    x_step(2, 0)
-    w_step(1, 1, 1)
-    w_step(1, 2, 0)
-    x_step(2, 1)
     w_step(1, 2, 1)
+    w_step(1, 3, 0)
     column_done(2)
     scale_column(2)
-    products(2, 0)
-    w_step(1, 3, 0)
     w_step(1, 3, 1)
     x_step(3, 0)
     x_step(3, 1)
+    products(2, 0)
     w_step(1, 4, 0)
     w_step(1, 4, 1)
     siblings_done(1)

time: 114 us -> 112 us (0.982)
  Pallas kernels: 112 us -> 110 us
    pallas_call x1, Pallas kernels: 112 us -> 110 us  [on_device(): pl.pallas_call(kernel, out_shape=jax.ShapeDtypeStruct((ROWS, CHAN), BF16)...]
where the time goes in v5:
time: 112 us
  Pallas kernels  110 us (98%)
  local copies, waits for them, and re-layouts  1.67 us (1%)
    pallas_call x1, Pallas kernels, on_device(): pl.pallas_call(kernel, out_shape=jax.ShapeDtypeStruct((ROWS, CHAN), BF16)...  110 us

profile of v5, /device:TPU:1, one launch (start us, length us, event | category | flops | bytes accessed | tf_op | source)
XLA Modules:
  0.0 111.6 jit_solution(11097085908582726756)
XLA Ops:
  0.0 109.9 %hyena.1 = bf16[512,256]{1,0:T(8,128)(2,1)} custom-call(bf16[512,512]{1,0:T(8,128)(2,1)} %tok.1, f32[1,8192]{1,0:T(1,128)} %bitcast.3, bf16[3,256,256]{2,1,0:T(8,128)(2,1)} %bitcast.2, f32[3,3,256]{2,1,0:T(4,128)} %sfilt.1, f32[128,256]{1,0:T(8,128)} %lfilt.1), custom_call_target="tpu_custom_call" | custom-call | tf_op jit(solution)/shard_map/hyena/pallas_call | solution.py:398
  110.0 1.7 %copy.7 = bf16[512,256]{1,0:T(8,128)(2,1)} copy(bf16[512,256]{1,0:T(8,128)(2,1)} %hyena.1) | data formatting | bytes 524288

commit v6 on v5

--- a/solution.py
+++ b/solution.py
@@ -229,7 +229,6 @@
             own_y(0, False)
         own_y(half, True)
     to_partner(0, True)
-    to_sibling(0, 0, True)
     local_t.start()
     local_w.start()
     acc[...] = jnp.zeros_like(acc)
@@ -256,6 +255,7 @@
     p_step(0)
     w_step(0, 4, 0)
     w_step(0, 4, 1)
+    to_sibling(0, 0, True)
     y_step(3, 0)
     p_step(1)
     w_step(1, 1, 0)

time: 112 us -> 112 us (level)
  no operation moved by 1% of the time
where the time goes in v6:
time: 112 us
  Pallas kernels  110 us (98%)
  local copies, waits for them, and re-layouts  1.67 us (1%)
    pallas_call x1, Pallas kernels, on_device(): pl.pallas_call(kernel, out_shape=jax.ShapeDtypeStruct((ROWS, CHAN), BF16)...  110 us

profile of v6, /device:TPU:1, one launch (start us, length us, event | category | flops | bytes accessed | tf_op | source)
XLA Modules:
  0.0 111.6 jit_solution(1651191914513745542)
XLA Ops:
  0.0 109.9 %hyena.1 = bf16[512,256]{1,0:T(8,128)(2,1)} custom-call(bf16[512,512]{1,0:T(8,128)(2,1)} %tok.1, f32[1,8192]{1,0:T(1,128)} %bitcast.3, bf16[3,256,256]{2,1,0:T(8,128)(2,1)} %bitcast.2, f32[3,3,256]{2,1,0:T(4,128)} %sfilt.1, f32[128,256]{1,0:T(8,128)} %lfilt.1), custom_call_target="tpu_custom_call" | custom-call | tf_op jit(solution)/shard_map/hyena/pallas_call | solution.py:398
  110.0 1.7 %copy.7 = bf16[512,256]{1,0:T(8,128)(2,1)} copy(bf16[512,256]{1,0:T(8,128)(2,1)} %hyena.1) | data formatting | bytes 524288
